TPU v7x, 256 devices: a whole 4x4x8 slice. The times are simulated.
256 devices in a mesh: view: 16 (over z, y_hi), tok: 16 (over y_lo, x, core).
Axes of the slice: x: 4, y: 4 (y_hi: 2, y_lo: 2; y = y_hi * 2 + y_lo), z: 8, core: 2. Of those that a mesh axis runs over, the one named last changes fastest.
Arguments:
- q1: bfloat16 [16, 512, 1024], P('view', 'tok'), may hold values from -96 to 96
- k1: bfloat16 [16, 512, 1024], P('view', 'tok'), may hold values from -6 to 6
- v1: bfloat16 [16, 512, 1024], P('view', 'tok'), may hold values from -6 to 6
- nbr: int32 [16, 7], P('view'), may hold values from 0 to 15, as said below
- x2: bfloat16 [16, 512, 1024], P('view', 'tok'), may hold values from -6 to 6
- w_view_out: bfloat16 [1024, 1024], replicated, may hold values from -0.1875 to 0.1875
- norm_gain: float32 [1024], replicated, may hold values from 0.5 to 1.5
- w_qkv: bfloat16 [1024, 3072], replicated, may hold values from -0.1875 to 0.1875
- w_out: bfloat16 [1024, 1024], replicated, may hold values from -0.1875 to 0.1875
Outputs:
- view_feats: float32 [16, 512, 1024], P('view', 'tok')
- lrm_out: float32 [16, 512, 1024], P('view', 'tok')
Inputs may be any that keep to these rules, and one draw needn't show every extreme that they name: `nbr`: row v lists 7 distinct view indices, none equal to v.
All inputs are finite; a program needn't handle non-finite values.
Results may differ from a plain program's by a relative error of at most 0.014.
Values may be sent and summed in bfloat16 or wider, within the bound.
A program may use at most 128 MiB of HBM per device.

v0:
```python
import jax
import jax.numpy as jnp
from jax import lax
from jax.sharding import PartitionSpec as P

H1 = 16
HD1 = 64
HD2 = 64
EPSILON = 1e-06
NEGATIVE = -1e30


def absorb(running, queries, key_piece, val_piece, keep_key, factor_scale):
    running_max, row_total, weighted = running
    scores = (
        jnp.einsum("qhd,khd->qhk", queries, key_piece, preferred_element_type=jnp.float32)
        * factor_scale
    )
    scores = jnp.where(keep_key[None, None, :], scores, NEGATIVE)
    new_max = jnp.maximum(running_max, jnp.max(scores, axis=-1))
    weights = jnp.where(keep_key[None, None, :], jnp.exp(scores - new_max[..., None]), 0.0)
    row_total = jnp.sum(weights, axis=-1)
    weighted = jnp.einsum(
        "qhk,khd->qhd", weights.astype(jnp.bfloat16), val_piece, preferred_element_type=jnp.float32
    )
    return (new_max, row_total, weighted)


def per_device(q1, k1, v1, nbr, x2, w_view_out, norm_gain, w_qkv, w_out):
    own_view = lax.axis_index("view")
    wanted = nbr[0]
    queries = lax.all_gather(q1, "tok", axis=1, tiled=True)[0].reshape(-1, H1, HD1)
    query_rows = queries.shape[0]
    start_state = (
        jnp.full((query_rows, H1), NEGATIVE, jnp.float32),
        jnp.zeros((query_rows, H1), jnp.float32),
        jnp.zeros((query_rows, H1, HD1), jnp.float32),
    )
    scale_one = HD1 ** (-0.5)
    key_piece = lax.all_gather(k1, "view", axis=0, tiled=True)
    val_piece = lax.all_gather(v1, "view", axis=0, tiled=True)
    view_ids = jnp.arange(key_piece.shape[0], dtype=jnp.int32)
    keep_view = (view_ids == own_view) | jnp.any(view_ids[:, None] == wanted[None, :], axis=1)
    keep_key = jnp.repeat(keep_view, key_piece.shape[1])
    running_max, row_total, weighted = absorb(
        start_state,
        queries,
        key_piece.reshape(-1, H1, HD1),
        val_piece.reshape(-1, H1, HD1),
        keep_key,
        scale_one,
    )
    tok_devs = lax.axis_size("tok")
    my_rows = query_rows // tok_devs
    row_peak = lax.pmax(running_max, "tok")
    factor = jnp.exp(running_max - row_peak)
    summed, totals = (
        lax.psum_scatter(weighted * factor[..., None], "tok", scatter_dimension=0, tiled=True),
        lax.psum_scatter(row_total * factor, "tok", scatter_dimension=0, tiled=True),
    )
    attn_one = (summed / totals[..., None]).reshape(my_rows, -1)
    features = attn_one * lax.rsqrt(jnp.mean(attn_one * attn_one, axis=-1, keepdims=True) + EPSILON)
    features_half = features.astype(jnp.bfloat16)
    hidden = x2[0].astype(jnp.float32) + jnp.dot(
        features_half, w_view_out, preferred_element_type=jnp.float32
    )
    normed = (
        hidden * lax.rsqrt(jnp.mean(hidden * hidden, axis=-1, keepdims=True) + EPSILON) * norm_gain
    ).astype(jnp.bfloat16)
    projected = (
        jnp.dot(normed, w_qkv, preferred_element_type=jnp.float32)
        .astype(jnp.bfloat16)
        .reshape(my_rows, 3, -1)
    )
    by_head = lax.all_to_all(projected, "tok", split_axis=2, concat_axis=0, tiled=True)
    local_heads = by_head.shape[2] // HD2
    head_queries = by_head[:, 0].reshape(-1, local_heads, HD2)
    view_rows = head_queries.shape[0]
    scale_two = HD2 ** (-0.5)
    second_state = (
        jnp.full((view_rows, local_heads), NEGATIVE, jnp.float32),
        jnp.zeros((view_rows, local_heads), jnp.float32),
        jnp.zeros((view_rows, local_heads, HD2), jnp.float32),
    )
    key_piece = lax.all_gather(by_head[:, 1], "view", axis=0, tiled=True)
    val_piece = lax.all_gather(by_head[:, 2], "view", axis=0, tiled=True)
    keep_key = jnp.ones((key_piece.shape[0],), jnp.bool_)
    second_max, second_total, second_sum = absorb(
        second_state,
        head_queries,
        key_piece.reshape(-1, local_heads, HD2),
        val_piece.reshape(-1, local_heads, HD2),
        keep_key,
        scale_two,
    )
    attn_two = (second_sum / second_total[..., None]).reshape(view_rows, -1).astype(jnp.bfloat16)
    returned = lax.all_to_all(attn_two, "tok", split_axis=0, concat_axis=1, tiled=True)
    wide = returned.astype(jnp.float32)
    unit_rows = (wide * lax.rsqrt(jnp.mean(wide * wide, axis=-1, keepdims=True) + EPSILON)).astype(
        jnp.bfloat16
    )
    result = jnp.dot(unit_rows, w_out, preferred_element_type=jnp.float32)
    return (features[None], result[None])


def solution(mesh):
    return jax.shard_map(
        per_device,
        mesh=mesh,
        in_specs=(
            P("view", "tok", None),
            P("view", "tok", None),
            P("view", "tok", None),
            P("view", None),
            P("view", "tok", None),
            P(),
            P(),
            P(),
            P(),
        ),
        out_specs=(P("view", "tok", None), P("view", "tok", None)),
        check_vma=False,
    )
```

profile of v0, /device:TPU:1, one launch (start us, length us, event | category | flops | bytes accessed | tf_op | source)
XLA Modules:
  0.0 568.1 jit_solution(11776893962329701940)
XLA Ops:
  7.2 0.7 all-gather.8.cloned.1.call-update
  8.0 0.7 all-gather.10.cloned.1.call-update
  8.7 0.7 all-gather.12.cloned.1.call-update
  9.4 0.7 fusion.49
  10.3 0.1 broadcast_in_dim.58
  10.4 78.4 %all-gather.8.cloned.1.call-done = bf16[16,32,1024]{2,1,0:T(8,128)(2,1)} async-done(((bf16[1,32,1024]{2,1,0:T(8,128)(2,1)}), bf16[16,32,1024]{2,1,0:T(8,128)(2,1)}) %all-gather.8.cloned.1.call-update) | async-done | bytes 1048592 | tf_op jit(solution)/shard_map/all_gather | solution.py:40
  88.8 4.1 reshape.120
  92.8 33.8 %all-gather.10.cloned.1.call-done = bf16[1,512,1024]{2,1,0:T(8,128)(2,1)} async-done(((bf16[1,32,1024]{2,1,0:T(8,128)(2,1)}), bf16[1,512,1024]{2,1,0:T(8,128)(2,1)}) %all-gather.10.cloned.1.call-update) | async-done | bytes 1048592 | tf_op jit(solution)/shard_map/all_gather | solution.py:32
  126.6 1.5 copy.56
  128.1 9.1 %bitcast_reduce_fusion = (f32[512,16]{0,1:T(8,128)S(1)}, f32[16,512,512]{2,1,0:T(8,128)}) fusion(pred[512]{0:T(512)(128)(4,1)S(1)} %broadcast_in_dim.58, bf16[512,16,64]{0,2,1:T(8,128)(2,1)S(1)} %bitcast.104, bf16[512,16,64]{2,1,0:T(8,128)(2,1)} %reshape.120), kind=kOutput, calls=%fused_computation.3 | convolution fusion | flops 549445632 | bytes 18907648 | tf_op jit(solution)/shard_map/qhd,khd->qhk/dot_general | solution.py:16
  137.2 50.7 %pmax.7 = f32[512,16]{0,1:T(8,128)S(1)} all-reduce(f32[512,16]{0,1:T(8,128)S(1)} %broadcast_maximum_fusion), channel_id=1, replica_groups=mesh['view'=16,'tok'=16] {'tok'}, use_global_device_ids=true, to_apply=%region_2.3 | all-reduce | flops 8192 | bytes 65536 | tf_op jit(solution)/shard_map/pmax | solution.py:55
  187.8 8.2 %fusion.5 = f32[512,16]{0,1:T(8,128)S(1)} fusion(f32[16,512,512]{2,1,0:T(8,128)} %get-tuple-element.9, f32[512,16]{0,1:T(8,128)S(1)} %broadcast_maximum_fusion, pred[512]{0:T(512)(128)(4,1)S(1)} %broadcast_in_dim.58), kind=kLoop, calls=%fused_computation.10 | loop fusion | flops 20963328 | bytes 16843264 | tf_op jit(solution)/shard_map/reduce_sum | solution.py:22
  196.0 0.8 copy.73
  196.9 6.2 %all-gather.12.cloned.1.call-done = bf16[16,32,1024]{2,1,0:T(8,128)(2,1)} async-done(((bf16[1,32,1024]{2,1,0:T(8,128)(2,1)}), bf16[16,32,1024]{2,1,0:T(8,128)(2,1)}) %all-gather.12.cloned.1.call-update) | async-done | bytes 1048592 | tf_op jit(solution)/shard_map/all_gather | solution.py:41
  203.1 4.1 reshape.121
  207.1 11.6 %bitcast_multiply_fusion = f32[512,16,64]{0,2,1:T(8,128)} fusion(f32[16,512,512]{2,1,0:T(8,128)} %get-tuple-element.9, f32[512,16]{0,1:T(8,128)S(1)} %broadcast_maximum_fusion, pred[512]{0:T(512)(128)(4,1)S(1)} %broadcast_in_dim.58, bf16[512,16,64]{2,1,0:T(8,128)(2,1)} %reshape.121, f32[512,16]{0,1:T(8,128)S(1)} %get-tuple-element.5), kind=kOutput, calls=%fused_computation.21 | convolution fusion | flops 558366720 | bytes 19988992 | tf_op jit(solution)/shard_map/qhk,khd->qhd/dot_general | solution.py:23
  218.8 4.8 copy.60
  223.6 0.2 all-gather.16.cloned.1.call-start
  223.9 42.9 %reduce-scatter.7.cloned.1.call-done = f32[32,16]{1,0:T(8,128)} async-done(((f32[512,16]{1,0:T(8,128)}), f32[32,16]{1,0:T(8,128)}) %reduce-scatter.7.cloned.1.call-update) | async-done | bytes 2064 | tf_op jit(solution)/shard_map/reduce_scatter | solution.py:59
  266.7 70.7 %reduce-scatter.5.cloned.1.call-done = f32[32,16,64]{2,1,0:T(8,128)} async-done(((f32[512,16,64]{2,1,0:T(8,128)}), f32[32,16,64]{2,1,0:T(8,128)}) %reduce-scatter.5.cloned.1.call-update) | async-done | bytes 131088 | tf_op jit(solution)/shard_map/reduce_scatter | solution.py:58
  337.4 1.5 multiply_reduce_fusion.1
  338.9 0.1 reshape.123
  339.1 0.6 multiply_reduce_fusion.2
  339.7 4.0 convolution_convert_fusion
  343.7 1.0 reshape.124
  344.7 1.8 copy.62
  346.5 1.4 reshape.133
  347.9 14.7 %all_to_all.28 = bf16[16,2,3072]{2,1,0:T(2,128)(2,1)} all-to-all(bf16[16,2,3072]{2,1,0:T(2,128)(2,1)} %reshape.133), channel_id=1, replica_groups=mesh['view'=16,'tok'=16] {'tok'}, dimensions={0} | all-to-all | bytes 393216 | tf_op jit(solution)/shard_map/all_to_all | solution.py:75
  362.6 1.6 reshape.134
  364.2 1.3 copy.72
  365.4 1.7 fusion.55
  367.2 0.7 all-gather.14.cloned.1.call-update
  367.9 0.1 reshape.122
  368.0 79.9 %all-gather.16.cloned.1.call-done = bf16[8192,1,64]{2,0,1:T(8,128)(2,1)} async-done(((bf16[512,1,64]{2,0,1:T(8,128)(2,1)}), bf16[8192,1,64]{2,0,1:T(8,128)(2,1)}) %all-gather.16.cloned.1.call-update) | async-done | bytes 1048592 | tf_op jit(solution)/shard_map/all_gather | solution.py:85
  447.9 9.6 %multiply_reduce_fusion = (f32[512]{0:T(512)S(1)}, f32[8192,512]{1,0:T(8,128)}) fusion(bf16[512,3,64]{2,0,1:T(8,128)(2,1)} %bitcast.108, bf16[8192,1,64]{2,0,1:T(8,128)(2,1)} %all-gather.16.cloned.1.call-done), kind=kOutput, calls=%fused_computation.7 | convolution fusion | flops 545259008 | bytes 19007488 | tf_op jit(solution)/shard_map/qhd,khd->qhk/dot_general | solution.py:16
  457.6 8.6 %fusion.3 = f32[512]{0:T(512)S(1)} fusion(f32[8192,512]{1,0:T(8,128)} %get-tuple-element.13, f32[512]{0:T(512)S(1)} %broadcast_maximum_fusion.1), kind=kLoop, calls=%fused_computation.8 | loop fusion | flops 12582400 | bytes 16781312 | tf_op jit(solution)/shard_map/reduce_sum | solution.py:22
  466.2 67.0 %all-gather.14.cloned.1.call-done = bf16[8192,1,64]{2,0,1:T(8,128)(2,1)} async-done(((bf16[512,1,64]{2,0,1:T(8,128)(2,1)}), bf16[8192,1,64]{2,0,1:T(8,128)(2,1)}) %all-gather.14.cloned.1.call-update) | async-done | bytes 1048592 | tf_op jit(solution)/shard_map/all_gather | solution.py:86
  533.2 9.3 %fusion.39 = bf16[512,1,64]{0,2,1:T(8,128)(2,1)S(1)} fusion(f32[8192,512]{1,0:T(8,128)} %get-tuple-element.13, f32[512]{0:T(512)S(1)} %broadcast_maximum_fusion.1, bf16[8192,1,64]{2,0,1:T(8,128)(2,1)} %all-gather.14.cloned.1.call-done, f32[512]{0:T(512)S(1)} %fusion.3), kind=kOutput, calls=%fused_computation.30 | convolution fusion | flops 549519360 | bytes 17895424 | tf_op jit(solution)/shard_map/qhk,khd->qhd/dot_general | solution.py:23
  542.5 0.1 copy.68
  542.7 0.8 reshape.135
  543.4 8.6 %all-to-all-start.1 = ((bf16[16,2,1024]{2,1,0:T(2,128)(2,1)}), bf16[16,2,1024]{2,1,0:T(2,128)(2,1)S(1)}, u32[]{:S(2)}, u32[]{:S(2)}) async-start(bf16[16,2,1024]{2,1,0:T(2,128)(2,1)} %reshape.135), calls=%async_computation.2 | async-start | bytes 131072 | tf_op jit(solution)/shard_map/all_to_all | solution.py:97
  552.0 0.7 broadcast_multiply_fusion
  552.8 5.1 all-to-all-done.1
  557.8 0.1 reshape.136
  558.0 0.1 fusion.44
  558.2 0.2 copy.69
  558.3 0.1 reshape.128
  558.5 2.8 convolution_bitcast_fusion
  (24 shorter events, 0.5 us)
Async XLA Ops:
  7.2 331.9 %copy-start = (bf16[1024,1024]{1,0:T(8,128)(2,1)S(1)}, bf16[1024,1024]{1,0:T(8,128)(2,1)}, u32[]{:S(2)}) copy-start(bf16[1024,1024]{1,0:T(8,128)(2,1)} %param.14) | copy-start | bytes 6291460
  7.2 81.6 %all-gather.8.cloned.1.call-start = ((), (), s32[]{:S(2)}) async-start(), calls=%async_computation.4 | async-start | bytes 1114112 | tf_op jit(solution)/shard_map/all_gather | solution.py:40
  7.9 118.7 %all-gather.10.cloned.1.call-start = ((), (), s32[]{:S(2)}) async-start(), calls=%async_computation.5 | async-start | bytes 1114112 | tf_op jit(solution)/shard_map/all_gather | solution.py:32
  8.7 194.4 %all-gather.12.cloned.1.call-start = ((), (), s32[]{:S(2)}) async-start(), calls=%async_computation.6 | async-start | bytes 1114112 | tf_op jit(solution)/shard_map/all_gather | solution.py:41
  9.4 257.3 %reduce-scatter.7.cloned.1.call-start = ((), (), s32[]{:S(2)}) async-start(), calls=%async_computation.10 | async-start | bytes 278528 | tf_op jit(solution)/shard_map/reduce_scatter | solution.py:59
  196.9 140.5 %reduce-scatter.5.cloned.1.call-start = ((), (), s32[]{:S(2)}) async-start(), calls=%async_computation.7 | async-start | bytes 4456448 | tf_op jit(solution)/shard_map/reduce_scatter | solution.py:58
  207.1 131.9 %copy-start.1 = (bf16[1,32,1024]{2,1,0:T(8,128)(2,1)S(1)}, bf16[1,32,1024]{2,1,0:T(8,128)(2,1)}, u32[]{:S(2)}) copy-start(bf16[1,32,1024]{2,1,0:T(8,128)(2,1)} %param.13) | copy-start | bytes 196612
  207.1 132.6 %copy-start.2 = (f32[1024]{0:T(1024)S(1)}, f32[1024]{0:T(1024)}, u32[]{:S(2)}) copy-start(f32[1024]{0:T(1024)} %param.15) | copy-start | bytes 12292
  223.6 224.3 %all-gather.16.cloned.1.call-start = ((), (), s32[]{:S(2)}) async-start(), calls=%async_computation.9 | async-start | bytes 2228224 | tf_op jit(solution)/shard_map/all_gather | solution.py:85
  367.1 166.1 %all-gather.14.cloned.1.call-start = ((), (), s32[]{:S(2)}) async-start(), calls=%async_computation.8 | async-start | bytes 2228224 | tf_op jit(solution)/shard_map/all_gather | solution.py:86
  543.4 14.4 %all-to-all-start.1 = ((bf16[16,2,1024]{2,1,0:T(2,128)(2,1)}), bf16[16,2,1024]{2,1,0:T(2,128)(2,1)S(1)}, u32[]{:S(2)}, u32[]{:S(2)}) async-start(bf16[16,2,1024]{2,1,0:T(2,128)(2,1)} %reshape.135), calls=%async_computation.2 | async-start | bytes 131072 | tf_op jit(solution)/shard_map/all_to_all | solution.py:97
Sparse Core Ops, SparseCore 0:
  10.6 78.1 all-gather.7
  90.6 35.9 all-gather.9
  129.2 73.8 all-gather.11
  205.4 61.2 reduce-scatter.6
  269.1 68.2 reduce-scatter.4
  367.3 80.6 all-gather.15
  451.1 82.0 all-gather.13
where the time goes:
time: 569 us; the launch traced here: 568 us
  waiting for transfers between devices  387 us (68%)
  blocking collectives  65.4 us (11%)
  matrix products  47.1 us (8%)
  local copies, waits for them, and re-layouts  25.7 us (5%)
  other arithmetic  20 us (4%)
  between operations  14.3 us (3%)
  starting transfers between devices  9.04 us (2%)
    all_gather x1, waiting for transfers between devices, per_device(): key_piece = lax.all_gather(by_head[:, 1], 'view', axis=0, tiled=True)  79.9 us
    all_gather x1, waiting for transfers between devices, per_device(): key_piece = lax.all_gather(k1, 'view', axis=0, tiled=True)  78.4 us
    reduce_scatter x1, waiting for transfers between devices, per_device(): lax.psum_scatter(weighted * factor[..., None], 'tok', scatter_dimension=0...  70.7 us
    all_gather x1, waiting for transfers between devices, per_device(): val_piece = lax.all_gather(by_head[:, 2], 'view', axis=0, tiled=True)  67 us
    pmax x1, blocking collectives, per_device(): row_peak = lax.pmax(running_max, 'tok')  50.7 us
    reduce_scatter x1, waiting for transfers between devices, per_device(): lax.psum_scatter(row_total * factor, 'tok', scatter_dimension=0, tiled=True)  42.9 us
    all_gather x1, waiting for transfers between devices, per_device(): lax.all_gather(q1, 'tok', axis=1, tiled=True)[0].reshape(-1, H1, HD1)  33.8 us
    dot_general x2, matrix products, absorb(): jnp.einsum('qhk,khd->qhd', weights.astype(jnp.bfloat16), val_piece, prefe...  21 us
  transfers between devices with their start and end apart: 8, of which 8 were waited for; matrix products, arithmetic and copies ran while one was open for 11% of the time, Pallas kernels for 0%

commit v1 on v0

--- a/solution.py
+++ b/solution.py
@@ -37,8 +37,18 @@
         jnp.zeros((query_rows, H1, HD1), jnp.float32),
     )
     scale_one = HD1 ** (-0.5)
-    key_piece = lax.all_gather(k1, "view", axis=0, tiled=True)
-    val_piece = lax.all_gather(v1, "view", axis=0, tiled=True)
+
+    def handle_sums_all_up(arr, local_block, shard_axis="view"):
+        front = jnp.split(
+            lax.all_gather(
+                jnp.concatenate([arr, local_block], 1), axis_name=shard_axis, axis=0, tiled=True
+            ),
+            [arr.shape[1]],
+            1,
+        )
+        return front
+
+    key_piece, val_piece = handle_sums_all_up(k1, v1)
     view_ids = jnp.arange(key_piece.shape[0], dtype=jnp.int32)
     keep_view = (view_ids == own_view) | jnp.any(view_ids[:, None] == wanted[None, :], axis=1)
     keep_key = jnp.repeat(keep_view, key_piece.shape[1])

time: 569 us -> 574 us (level)
    all_gather x2 -> x1, waiting for transfers between devices: 84.5 us -> 83 us  [handle_sums_all_up(): lax.all_gather(jnp.concatenate([arr, local_block], 1), axis_name=shard_ax...]
  transfers between devices with their start and end apart: 8 -> 7, of which waited for: 8 -> 7; matrix products, arithmetic and copies ran while one was open for 11% -> 7% of each run, Pallas kernels for 0% -> 0%
where the time goes in v1:
time: 574 us
  waiting for transfers between devices  387 us (67%)
  blocking collectives  67.4 us (12%)
  matrix products  47.1 us (8%)
  local copies, waits for them, and re-layouts  27.2 us (5%)
  other arithmetic  21.5 us (4%)
  between operations  14.2 us (2%)
  starting transfers between devices  9.01 us (2%)
    all_gather x1, waiting for transfers between devices, handle_sums_all_up(): lax.all_gather(jnp.concatenate([arr, local_block], 1), axis_name=shard_ax...  83 us
    all_gather x1, waiting for transfers between devices, per_device(): key_piece = lax.all_gather(by_head[:, 1], 'view', axis=0, tiled=True)  80.1 us
    reduce_scatter x1, waiting for transfers between devices, per_device(): lax.psum_scatter(weighted * factor[..., None], 'tok', scatter_dimension=0...  70.6 us
    all_gather x1, waiting for transfers between devices, per_device(): val_piece = lax.all_gather(by_head[:, 2], 'view', axis=0, tiled=True)  66.9 us
    pmax x1, blocking collectives, per_device(): row_peak = lax.pmax(running_max, 'tok')  52.7 us
    reduce_scatter x1, waiting for transfers between devices, per_device(): lax.psum_scatter(row_total * factor, 'tok', scatter_dimension=0, tiled=True)  42 us
    all_gather x1, waiting for transfers between devices, per_device(): lax.all_gather(q1, 'tok', axis=1, tiled=True)[0].reshape(-1, H1, HD1)  38.3 us
    dot_general x2, matrix products, absorb(): jnp.einsum('qhk,khd->qhd', weights.astype(jnp.bfloat16), val_piece, prefe...  21 us
  transfers between devices with their start and end apart: 7, of which 7 were waited for; matrix products, arithmetic and copies ran while one was open for 7% of the time, Pallas kernels for 0%

profile of v1, /device:TPU:1, one launch (start us, length us, event | category | flops | bytes accessed | tf_op | source)
XLA Modules:
  0.0 573.7 jit_solution(1088139318868740372)
XLA Ops:
  7.2 0.7 all-gather.9.cloned.1.call-update
  8.0 1.5 pad_maximum_fusion
  9.6 0.7 fusion.49
  10.3 0.1 broadcast_in_dim.57
  10.4 0.1 broadcast_in_dim.58
  10.5 38.3 %all-gather.9.cloned.1.call-done = bf16[1,512,1024]{2,1,0:T(8,128)(2,1)} async-done(((bf16[1,32,1024]{2,1,0:T(8,128)(2,1)}), bf16[1,512,1024]{2,1,0:T(8,128)(2,1)}) %all-gather.9.cloned.1.call-update) | async-done | bytes 1048592 | tf_op jit(solution)/shard_map/all_gather | solution.py:32
  48.8 1.5 copy.56
  50.3 83.0 %all-gather.7.cloned.1.call-done = bf16[16,64,1024]{2,1,0:T(8,128)(2,1)} async-done(((bf16[1,64,1024]{2,1,0:T(8,128)(2,1)}), bf16[16,64,1024]{2,1,0:T(8,128)(2,1)}) %all-gather.7.cloned.1.call-update) | async-done | bytes 2097168 | tf_op jit(solution)/shard_map/all_gather | solution.py:43
  133.3 3.2 fusion.55
  136.5 4.1 reshape.121
  140.5 9.1 %bitcast_reduce_fusion = (f32[512,16]{0,1:T(8,128)S(1)}, f32[16,512,512]{2,1,0:T(8,128)}) fusion(pred[512]{0:T(512)(128)(4,1)S(1)} %broadcast_in_dim.58, bf16[512,16,64]{0,2,1:T(8,128)(2,1)S(1)} %bitcast.104, bf16[512,16,64]{2,1,0:T(8,128)(2,1)} %reshape.121), kind=kOutput, calls=%fused_computation.3 | convolution fusion | flops 549445632 | bytes 18907648 | tf_op jit(solution)/shard_map/qhd,khd->qhk/dot_general | solution.py:16
  149.6 52.7 %pmax.7 = f32[512,16]{0,1:T(8,128)S(1)} all-reduce(f32[512,16]{0,1:T(8,128)S(1)} %broadcast_maximum_fusion), channel_id=1, replica_groups=mesh['view'=16,'tok'=16] {'tok'}, use_global_device_ids=true, to_apply=%region_2.3 | all-reduce | flops 8192 | bytes 65536 | tf_op jit(solution)/shard_map/pmax | solution.py:65
  202.3 8.2 %fusion.5 = f32[512,16]{0,1:T(8,128)S(1)} fusion(f32[16,512,512]{2,1,0:T(8,128)} %get-tuple-element.11, f32[512,16]{0,1:T(8,128)S(1)} %broadcast_maximum_fusion, pred[512]{0:T(512)(128)(4,1)S(1)} %broadcast_in_dim.58), kind=kLoop, calls=%fused_computation.10 | loop fusion | flops 20963328 | bytes 16843264 | tf_op jit(solution)/shard_map/reduce_sum | solution.py:22
  210.6 2.4 reshape.120
  213.0 0.8 copy.73
  213.9 11.6 %bitcast_multiply_fusion = f32[512,16,64]{0,2,1:T(8,128)} fusion(f32[16,512,512]{2,1,0:T(8,128)} %get-tuple-element.11, f32[512,16]{0,1:T(8,128)S(1)} %broadcast_maximum_fusion, pred[512]{0:T(512)(128)(4,1)S(1)} %broadcast_in_dim.58, bf16[512,16,64]{2,1,0:T(8,128)(2,1)} %reshape.120, f32[512,16]{0,1:T(8,128)S(1)} %get-tuple-element.5), kind=kOutput, calls=%fused_computation.21 | convolution fusion | flops 558366720 | bytes 19988992 | tf_op jit(solution)/shard_map/qhk,khd->qhd/dot_general | solution.py:23
  225.5 4.9 copy.60
  230.4 0.2 all-gather.13.cloned.1.call-start
  230.6 42.0 %reduce-scatter.7.cloned.1.call-done = f32[32,16]{1,0:T(8,128)} async-done(((f32[512,16]{1,0:T(8,128)}), f32[32,16]{1,0:T(8,128)}) %reduce-scatter.7.cloned.1.call-update) | async-done | bytes 2064 | tf_op jit(solution)/shard_map/reduce_scatter | solution.py:69
  272.6 70.6 %reduce-scatter.5.cloned.1.call-done = f32[32,16,64]{2,1,0:T(8,128)} async-done(((f32[512,16,64]{2,1,0:T(8,128)}), f32[32,16,64]{2,1,0:T(8,128)}) %reduce-scatter.5.cloned.1.call-update) | async-done | bytes 131088 | tf_op jit(solution)/shard_map/reduce_scatter | solution.py:68
  343.2 1.5 multiply_reduce_fusion.1
  344.7 0.1 reshape.123
  344.8 0.6 multiply_reduce_fusion.2
  345.5 4.0 convolution_convert_fusion
  349.5 1.0 reshape.124
  350.5 1.8 copy.62
  352.2 1.4 reshape.133
  353.6 14.7 %all_to_all.28 = bf16[16,2,3072]{2,1,0:T(2,128)(2,1)} all-to-all(bf16[16,2,3072]{2,1,0:T(2,128)(2,1)} %reshape.133), channel_id=1, replica_groups=mesh['view'=16,'tok'=16] {'tok'}, dimensions={0} | all-to-all | bytes 393216 | tf_op jit(solution)/shard_map/all_to_all | solution.py:85
  368.3 1.6 reshape.134
  369.9 1.3 copy.72
  371.2 1.7 fusion.56
  372.9 0.5 all-gather.11.cloned.1.call-update
  373.5 0.1 reshape.122
  373.6 80.1 %all-gather.13.cloned.1.call-done = bf16[8192,1,64]{2,0,1:T(8,128)(2,1)} async-done(((bf16[512,1,64]{2,0,1:T(8,128)(2,1)}), bf16[8192,1,64]{2,0,1:T(8,128)(2,1)}) %all-gather.13.cloned.1.call-update) | async-done | bytes 1048592 | tf_op jit(solution)/shard_map/all_gather | solution.py:95
  453.7 9.6 %multiply_reduce_fusion = (f32[512]{0:T(512)S(1)}, f32[8192,512]{1,0:T(8,128)}) fusion(bf16[512,3,64]{2,0,1:T(8,128)(2,1)} %bitcast.108, bf16[8192,1,64]{2,0,1:T(8,128)(2,1)} %all-gather.13.cloned.1.call-done), kind=kOutput, calls=%fused_computation.7 | convolution fusion | flops 545259008 | bytes 19007488 | tf_op jit(solution)/shard_map/qhd,khd->qhk/dot_general | solution.py:16
  463.3 8.6 %fusion.3 = f32[512]{0:T(512)S(1)} fusion(f32[8192,512]{1,0:T(8,128)} %get-tuple-element.15, f32[512]{0:T(512)S(1)} %broadcast_maximum_fusion.1), kind=kLoop, calls=%fused_computation.8 | loop fusion | flops 12582400 | bytes 16781312 | tf_op jit(solution)/shard_map/reduce_sum | solution.py:22
  471.9 66.9 %all-gather.11.cloned.1.call-done = bf16[8192,1,64]{2,0,1:T(8,128)(2,1)} async-done(((bf16[512,1,64]{2,0,1:T(8,128)(2,1)}), bf16[8192,1,64]{2,0,1:T(8,128)(2,1)}) %all-gather.11.cloned.1.call-update) | async-done | bytes 1048592 | tf_op jit(solution)/shard_map/all_gather | solution.py:96
  538.8 9.3 %fusion.39 = bf16[512,1,64]{0,2,1:T(8,128)(2,1)S(1)} fusion(f32[8192,512]{1,0:T(8,128)} %get-tuple-element.15, f32[512]{0:T(512)S(1)} %broadcast_maximum_fusion.1, bf16[8192,1,64]{2,0,1:T(8,128)(2,1)} %all-gather.11.cloned.1.call-done, f32[512]{0:T(512)S(1)} %fusion.3), kind=kOutput, calls=%fused_computation.30 | convolution fusion | flops 549519360 | bytes 17895424 | tf_op jit(solution)/shard_map/qhk,khd->qhd/dot_general | solution.py:23
  548.1 0.1 copy.68
  548.3 0.8 reshape.135
  549.0 8.6 %all-to-all-start.1 = ((bf16[16,2,1024]{2,1,0:T(2,128)(2,1)}), bf16[16,2,1024]{2,1,0:T(2,128)(2,1)S(1)}, u32[]{:S(2)}, u32[]{:S(2)}) async-start(bf16[16,2,1024]{2,1,0:T(2,128)(2,1)} %reshape.135), calls=%async_computation.2 | async-start | bytes 131072 | tf_op jit(solution)/shard_map/all_to_all | solution.py:107
  557.6 0.7 broadcast_multiply_fusion
  558.4 5.1 all-to-all-done.1
  563.5 0.1 reshape.136
  563.6 0.1 fusion.44
  563.8 0.2 copy.69
  563.9 0.1 reshape.128
  564.1 2.8 convolution_bitcast_fusion
  (25 shorter events, 0.4 us)
Async XLA Ops:
  7.2 337.7 %copy-start = (bf16[1024,1024]{1,0:T(8,128)(2,1)S(1)}, bf16[1024,1024]{1,0:T(8,128)(2,1)}, u32[]{:S(2)}) copy-start(bf16[1024,1024]{1,0:T(8,128)(2,1)} %param.14) | copy-start | bytes 6291460
  7.2 41.6 %all-gather.9.cloned.1.call-start = ((), (), s32[]{:S(2)}) async-start(), calls=%async_computation.5 | async-start | bytes 1114112 | tf_op jit(solution)/shard_map/all_gather | solution.py:32
  7.9 125.3 %all-gather.7.cloned.1.call-start = ((), (), s32[]{:S(2)}) async-start(), calls=%async_computation.4 | async-start | bytes 2228224 | tf_op jit(solution)/shard_map/all_gather | solution.py:43
  9.5 263.1 %reduce-scatter.7.cloned.1.call-start = ((), (), s32[]{:S(2)}) async-start(), calls=%async_computation.9 | async-start | bytes 278528 | tf_op jit(solution)/shard_map/reduce_scatter | solution.py:69
  202.3 8.2 %copy-start.1 = (bf16[16,32,1024]{2,1,0:T(8,128)(2,1)S(1)}, bf16[16,32,1024]{2,1,0:T(8,128)(2,1)}, u32[]{:S(2)}) copy-start(bf16[16,32,1024]{2,1,0:T(8,128)(2,1)} %get-tuple-element.6) | copy-start | bytes 3145732
  213.8 129.4 %reduce-scatter.5.cloned.1.call-start = ((), (), s32[]{:S(2)}) async-start(), calls=%async_computation.6 | async-start | bytes 4456448 | tf_op jit(solution)/shard_map/reduce_scatter | solution.py:68
  225.5 119.3 %copy-start.2 = (bf16[1,32,1024]{2,1,0:T(8,128)(2,1)S(1)}, bf16[1,32,1024]{2,1,0:T(8,128)(2,1)}, u32[]{:S(2)}) copy-start(bf16[1,32,1024]{2,1,0:T(8,128)(2,1)} %param.13) | copy-start | bytes 196612
  225.5 120.0 %copy-start.3 = (f32[1024]{0:T(1024)S(1)}, f32[1024]{0:T(1024)}, u32[]{:S(2)}) copy-start(f32[1024]{0:T(1024)} %param.15) | copy-start | bytes 12292
  230.4 223.3 %all-gather.13.cloned.1.call-start = ((), (), s32[]{:S(2)}) async-start(), calls=%async_computation.8 | async-start | bytes 2228224 | tf_op jit(solution)/shard_map/all_gather | solution.py:95
  372.9 165.9 %all-gather.11.cloned.1.call-start = ((), (), s32[]{:S(2)}) async-start(), calls=%async_computation.7 | async-start | bytes 2228224 | tf_op jit(solution)/shard_map/all_gather | solution.py:96
  549.0 14.4 %all-to-all-start.1 = ((bf16[16,2,1024]{2,1,0:T(2,128)(2,1)}), bf16[16,2,1024]{2,1,0:T(2,128)(2,1)S(1)}, u32[]{:S(2)}, u32[]{:S(2)}) async-start(bf16[16,2,1024]{2,1,0:T(2,128)(2,1)} %reshape.135), calls=%async_computation.2 | async-start | bytes 131072 | tf_op jit(solution)/shard_map/all_to_all | solution.py:107
Sparse Core Ops, SparseCore 0:
  9.8 38.9 all-gather.8
  52.0 81.2 all-gather.6
  213.9 58.6 reduce-scatter.6
  275.0 68.1 reduce-scatter.4
  373.0 80.6 all-gather.12
  456.7 82.0 all-gather.10
